TPU v7x, 32 devices: a whole 2x2x4 slice. The times are simulated.
32 devices in a mesh: dom: 8 (over y, x, core), feat: 4 (over z).
Axes of the slice: x: 2, y: 2, z: 4, core: 2. Of those that a mesh axis runs over, the one named last changes fastest.
Arguments:
- node_x: bfloat16 [2048, 256], P('dom', 'feat'), may hold values from -24 to 24, as said below
- cotangent: bfloat16 [2048, 256], P('dom', 'feat'), may hold values from -6 to 6
- assign: int32 [2048], P('dom'), may hold values from 0 to 4095
- part_sizes: int32 [8], P('dom'), may hold values from 64 to 256, as said below
- w_query: bfloat16 [256, 256], replicated, may hold values from -0.375 to 0.375
- w_key: bfloat16 [256, 256], replicated, may hold values from -1.5 to 1.5
- w_value: bfloat16 [256, 256], replicated, may hold values from -0.75 to 0.75
- w_out: bfloat16 [256, 256], replicated, may hold values from -0.375 to 0.375
Outputs:
- result_out: bfloat16 [2048, 256], P('dom', 'feat')
- grad_x: bfloat16 [2048, 256], P('dom', 'feat')
Inputs may be any that keep to these rules, and one draw needn't show every extreme that they name: `node_x`: node features; in the hidden draw rows differ in scale. Partition p holds live nodes in its first part_sizes[p] slots; in every draw some partition is full.
All inputs are finite; a program needn't handle non-finite values.
Results may differ from a plain program's by a relative error of at most 0.006.
The roundings to bfloat16 on the way count: a program that leaves them out, or rounds other values in their place, can miss the bound.
Values may be sent and summed in bfloat16 or wider, within the bound.
A program may use at most 64 MiB of HBM per device.

v0:
```python
import jax
import jax.numpy as jnp
from jax import lax
from jax.sharding import PartitionSpec as P

HEADS = 4
CENTROIDS = 4096


def trans_dot(left, right):
    return lax.dot_general(
        left, right, (((1,), (1,)), ((), ())), preferred_element_type=jnp.float32
    )


def inner_dot(left, right):
    return lax.dot_general(
        left, right, (((0,), (0,)), ((), ())), preferred_element_type=jnp.float32
    )


def local(node_x, cotangent, assign, part_sizes, w_query, w_key, w_value, w_out):
    row_count, head_width = node_x.shape
    inv_root = 1.0 / head_width**0.5
    offset = lax.axis_index("feat") * head_width
    wq_rows = lax.dynamic_slice_in_dim(w_query, offset, head_width, 0)
    wq_cols = lax.dynamic_slice_in_dim(w_query, offset, head_width, 1)
    wkv_cols = jnp.concatenate(
        [
            lax.dynamic_slice_in_dim(w_key, offset, head_width, 1),
            lax.dynamic_slice_in_dim(w_value, offset, head_width, 1),
        ],
        axis=1,
    )
    wo_rows = lax.dynamic_slice_in_dim(w_out, offset, head_width, 0)
    wo_cols = lax.dynamic_slice_in_dim(w_out, offset, head_width, 1)
    wk_rows = lax.dynamic_slice_in_dim(w_key, offset, head_width, 0).reshape(
        head_width, HEADS, 1, head_width
    )
    wv_rows = lax.dynamic_slice_in_dim(w_value, offset, head_width, 0).reshape(
        head_width, HEADS, 1, head_width
    )
    stacked = jnp.concatenate([wk_rows, wv_rows], axis=2).reshape(
        head_width, HEADS * 2 * head_width
    )
    stacked = jnp.transpose(stacked)
    alive_rows = (jnp.arange(row_count, dtype=jnp.int32) < part_sizes[0]).astype(jnp.float32)[
        :, None
    ]
    x_piece = lax.all_gather(node_x, "feat", axis=1, tiled=True)
    grad_piece = lax.all_gather(cotangent, "feat", axis=1, tiled=True)
    query_sum = jnp.dot(x_piece, wq_cols, preferred_element_type=jnp.float32)
    grad_sum = trans_dot(grad_piece, wo_rows)
    query = query_sum.astype(jnp.bfloat16)
    g_attended = (alive_rows * grad_sum).astype(jnp.bfloat16)
    onehot = (
        (assign[:, None] == jnp.arange(CENTROIDS, dtype=jnp.int32)[None, :]) & (alive_rows > 0.0)
    ).astype(jnp.bfloat16)
    cent_sums = inner_dot(onehot, node_x)
    counts = jnp.sum(onehot.astype(jnp.float32), axis=0)
    owned_sums, owned_counts = (
        lax.psum_scatter(cent_sums, "dom", scatter_dimension=0, tiled=True),
        lax.psum_scatter(counts, "dom", scatter_dimension=0, tiled=True),
    )
    owned_cent = (owned_sums / (owned_counts + 1.0)[:, None]).astype(jnp.bfloat16)
    owned_full = lax.all_gather(owned_cent, "feat", axis=1, tiled=True)
    owned_kv = jnp.dot(owned_full, wkv_cols, preferred_element_type=jnp.float32).astype(
        jnp.bfloat16
    )
    key_value = lax.all_gather(owned_kv, "dom", axis=0, tiled=True)
    keys = key_value[:, :head_width]
    values = key_value[:, head_width:]
    quarter = row_count // 4
    block_ids = jnp.arange(4, dtype=jnp.int32)
    live_blocks = (part_sizes[0] + quarter - 1) // quarter

    def attend_block(query_block, grad_block):
        scores = trans_dot(query_block, keys) * inv_root
        probs = jax.nn.softmax(scores, axis=1)
        probs_low = probs.astype(jnp.bfloat16)
        attended = jnp.dot(probs_low, values, preferred_element_type=jnp.float32).astype(
            jnp.bfloat16
        )
        g_probs = trans_dot(grad_block, values)
        row_delta = jnp.sum(probs * g_probs, axis=1, keepdims=True)
        g_scores = (probs * (g_probs - row_delta) * inv_root).astype(jnp.bfloat16)
        g_query = jnp.dot(g_scores, keys, preferred_element_type=jnp.float32).astype(jnp.bfloat16)
        key_grad = inner_dot(g_scores, query_block)
        value_grad = inner_dot(probs_low, grad_block)
        return (jnp.concatenate([key_grad, value_grad], axis=1), attended, g_query)

    def skip_block(query_block, grad_block):
        return (
            jnp.zeros((CENTROIDS, 2 * head_width), jnp.float32),
            jnp.zeros(query_block.shape, jnp.bfloat16),
            jnp.zeros(query_block.shape, jnp.bfloat16),
        )

    def step_block(running, block_triple):
        query_block, grad_block, active = block_triple
        kv_part, attended, g_query = lax.cond(
            active, attend_block, skip_block, query_block, grad_block
        )
        return (running + kv_part, (attended, g_query))

    start_grads = jnp.zeros((CENTROIDS, 2 * head_width), jnp.float32)
    kv_sum, outputs = lax.scan(
        step_block,
        start_grads,
        (
            query.reshape(4, quarter, head_width),
            g_attended.reshape(4, quarter, head_width),
            block_ids < live_blocks,
        ),
    )
    attended = outputs[0].reshape(row_count, head_width)
    g_query = outputs[1].reshape(row_count, head_width)
    out_wide = jnp.dot(
        lax.all_gather(attended, "feat", axis=1, tiled=True),
        wo_cols,
        preferred_element_type=jnp.float32,
    )
    result_out = (alive_rows * out_wide).astype(jnp.bfloat16)
    owned_grads = lax.psum_scatter(kv_sum, "dom", scatter_dimension=0, tiled=True).astype(
        jnp.bfloat16
    )
    owned_cent_grad = jnp.dot(
        lax.all_gather(owned_grads, "feat", axis=1, tiled=True),
        stacked,
        preferred_element_type=jnp.float32,
    )
    owned_cent_grad = owned_cent_grad / (owned_counts + 1.0)[:, None]
    cent_grad = lax.all_gather(owned_cent_grad, "dom", axis=0, tiled=True)
    from_query = trans_dot(lax.all_gather(g_query, "feat", axis=1, tiled=True), wq_rows)
    grad_x = (from_query + alive_rows * jnp.take(cent_grad, assign, axis=0)).astype(jnp.bfloat16)
    return (result_out, grad_x)


def solution(mesh):
    placed = (P("dom", "feat"), P("dom", "feat"), P("dom"), P("dom"), P(), P(), P(), P())
    return jax.shard_map(
        local,
        mesh=mesh,
        in_specs=placed,
        out_specs=(P("dom", "feat"), P("dom", "feat")),
        check_vma=False,
    )
```

profile of v0, /device:TPU:0, one launch (start us, length us, event | category | flops | bytes accessed | tf_op | source)
XLA Modules:
  0.0 230.0 jit_solution(8897731231757652999)
XLA Ops:
  8.1 2.9 %fusion.25 = f32[4096,64]{0,1:T(8,128)} fusion(bf16[256,64]{0,1:T(8,128)(2,1)} %param.12, s32[256]{0:T(256)} %param.14, pred[256]{0:T(512)(128)(4,1)S(1)} %broadcast_compare_fusion), kind=kOutput, calls=%fused_computation.36 | convolution fusion | flops 136314880 | bytes 1082624 | tf_op jit(solution)/shard_map/dot_general | solution.py:17
  12.3 1.0 convert_reduce_fusion
  13.3 25.9 %all-reduce = f32[4096]{0:T(1024)S(1)} all-reduce(f32[4096]{0:T(1024)S(1)} %convert_reduce_fusion), channel_id=3, replica_groups=mesh['dom'=8,'feat'=4] {'dom'}, use_global_device_ids=true, to_apply=%region_2.0.clone | all-reduce | flops 4096 | bytes 32768
  39.3 10.6 %reduce-scatter.3.cloned.1.call-done = f32[512,64]{0,1:T(8,128)} async-done(((f32[4096,64]{0,1:T(8,128)}), f32[512,64]{0,1:T(8,128)}) %reduce-scatter.3.cloned.1.call-update) | async-done | bytes 131088 | tf_op jit(solution)/shard_map/reduce_scatter | solution.py:62
  50.0 0.9 divide_convert_fusion
  50.9 13.8 %all_gather.25 = bf16[512,256]{0,1:T(8,128)(2,1)S(1)} all-gather(bf16[512,64]{0,1:T(8,128)(2,1)S(1)} %divide_convert_fusion), channel_id=1, replica_groups=mesh['dom'=8,'feat'=4] {'feat'}, dimensions={1}, use_global_device_ids=true | all-gather | bytes 327680 | tf_op jit(solution)/shard_map/all_gather | solution.py:66
  64.7 1.0 convolution_convert_fusion.2
  65.8 13.5 %all_gather.27 = bf16[256,256]{0,1:T(8,128)(2,1)S(1)} all-gather(bf16[256,64]{0,1:T(8,128)(2,1)S(1)} %copy-done.8), channel_id=1, replica_groups=mesh['dom'=8,'feat'=4] {'feat'}, dimensions={1}, use_global_device_ids=true | all-gather | bytes 163840 | tf_op jit(solution)/shard_map/all_gather | solution.py:51
  79.5 0.7 copy.38
  80.2 13.5 %all_gather.24 = bf16[256,256]{0,1:T(8,128)(2,1)S(1)} all-gather(bf16[256,64]{0,1:T(8,128)(2,1)S(1)} %copy-done.9), channel_id=1, replica_groups=mesh['dom'=8,'feat'=4] {'feat'}, dimensions={1}, use_global_device_ids=true | all-gather | bytes 163840 | tf_op jit(solution)/shard_map/all_gather | solution.py:50
  94.1 2.9 %fusion.47 = (bf16[4096,64]{1,0:T(8,128)(2,1)}, bf16[4096,64]{1,0:T(8,128)(2,1)S(1)}) fusion(bf16[4096,128]{1,0:T(8,128)(2,1)} %all-gather.3.cloned.1.call-done), kind=kLoop, calls=%fused_computation.76 | loop fusion | bytes 2097152 | tf_op jit(solution)/shard_map/slice | solution.py:72
  97.0 27.4 %while.15 = (s32[]{:T(128)}, f32[4096,128]{0,1:T(8,128)}, bf16[4,64,64]{2,1,0:T(8,128)(2,1)}, bf16[4,64,64]{2,1,0:T(8,128)(2,1)}, pred[4]{0:T(512)(128)(4,1)S(1)...) while((s32[]{:T(128)}, f32[4096,128]{0,1:T(8,128)}, ...), condition=%wide.region_9.10_spmd.clone, body=%wide.region_3.9_spmd.clone.sunk | while | flops 208150336 | bytes 28054544 | solution.py:107
  97.0 0.6 dynamic_slice.87
  98.3 4.2 %conditional.3 = (f32[4096,128]{0,1:T(8,128)S(1)}, bf16[1,64,64]{2,1,0:T(8,128)(2,1)S(1)}, bf16[1,64,64]{2,1,0:T(8,128)(2,1)S(1)}) conditional(s32[]{:T(128)} %bitcast.44, () %tuple.59, (bf16[4,64,64]{2,1,0:T(8,128)(2,1)S(1)}, s32[]{:T(128)}, bf16[4096,64]{1,0:T(8,128)(2,1)S(1)}, bf16[4,64,64]{2,1,0:T(8,128)(2,1)}, bf16[4096,64]{1,0:T(8,128)(2,1)}) %tuple.60), branch_computations={%region_4.4_spmd, %region_5.8_spmd} | conditional | flops 207101760 | bytes 21713248 | solution.py:101
  102.5 1.6 select_add_fusion.2
  104.7 0.6 dynamic_slice.87
  105.9 4.2 %conditional.3 = (f32[4096,128]{0,1:T(8,128)S(1)}, bf16[1,64,64]{2,1,0:T(8,128)(2,1)S(1)}, bf16[1,64,64]{2,1,0:T(8,128)(2,1)S(1)}) conditional(s32[]{:T(128)} %bitcast.44, () %tuple.59, (bf16[4,64,64]{2,1,0:T(8,128)(2,1)S(1)}, s32[]{:T(128)}, bf16[4096,64]{1,0:T(8,128)(2,1)S(1)}, bf16[4,64,64]{2,1,0:T(8,128)(2,1)}, bf16[4096,64]{1,0:T(8,128)(2,1)}) %tuple.60), branch_computations={%region_4.4_spmd, %region_5.8_spmd} | conditional | flops 207101760 | bytes 21713248 | solution.py:101
  110.2 3.1 %select_add_fusion.2 = f32[4096,128]{0,1:T(8,128)} fusion(f32[4096,128]{0,1:T(8,128)S(1)} %get-tuple-element.273, f32[4096,128]{0,1:T(8,128)} %get-tuple-element.296, pred[]{:T(512)S(6)} %compare.5), kind=kLoop, calls=%fused_computation.29.clone.1 | loop fusion | flops 1048576 | bytes 6291457 | tf_op jit(solution)/shard_map/while/body/eval_jaxpr/add | solution.py:104
  113.9 0.6 dynamic_slice.87
  115.4 3.1 %select_add_fusion.2 = f32[4096,128]{0,1:T(8,128)} fusion(f32[4096,128]{0,1:T(8,128)S(1)} %get-tuple-element.273, f32[4096,128]{0,1:T(8,128)} %get-tuple-element.296, pred[]{:T(512)S(6)} %compare.5), kind=kLoop, calls=%fused_computation.29.clone.1 | loop fusion | flops 1048576 | bytes 6291457 | tf_op jit(solution)/shard_map/while/body/eval_jaxpr/add | solution.py:104
  120.7 3.1 %select_add_fusion.2 = f32[4096,128]{0,1:T(8,128)} fusion(f32[4096,128]{0,1:T(8,128)S(1)} %get-tuple-element.273, f32[4096,128]{0,1:T(8,128)} %get-tuple-element.296, pred[]{:T(512)S(6)} %compare.5), kind=kLoop, calls=%fused_computation.29.clone.1 | loop fusion | flops 1048576 | bytes 6291457 | tf_op jit(solution)/shard_map/while/body/eval_jaxpr/add | solution.py:104
  124.5 0.8 constant_dynamic-slice_fusion
  125.9 48.4 %reduce-scatter.5.cloned.1.call-done = f32[512,128]{0,1:T(8,128)} async-done(((f32[4096,128]{0,1:T(8,128)}), f32[512,128]{0,1:T(8,128)}) %reduce-scatter.5.cloned.1.call-update) | async-done | bytes 262160 | tf_op jit(solution)/shard_map/reduce_scatter | solution.py:124
  174.3 1.0 convert_element_type.79
  175.3 15.4 %all_gather.30 = bf16[512,512]{0,1:T(8,128)(2,1)S(1)} all-gather(bf16[512,128]{0,1:T(8,128)(2,1)S(1)} %convert_element_type.79), channel_id=1, replica_groups=mesh['dom'=8,'feat'=4] {'feat'}, dimensions={1}, use_global_device_ids=true | all-gather | bytes 655360 | tf_op jit(solution)/shard_map/all_gather | solution.py:128
  190.7 0.9 convolution_divide_fusion
  191.9 13.9 %all_gather.28 = bf16[256,256]{0,1:T(8,128)(2,1)S(1)} all-gather(bf16[256,64]{0,1:T(8,128)(2,1)S(1)} %copy.39), channel_id=1, replica_groups=mesh['dom'=8,'feat'=4] {'feat'}, dimensions={1}, use_global_device_ids=true | all-gather | bytes 163840 | tf_op jit(solution)/shard_map/all_gather | solution.py:119
  205.8 13.3 %all_gather.29 = bf16[256,256]{0,1:T(8,128)(2,1)S(1)} all-gather(bf16[256,64]{0,1:T(8,128)(2,1)S(1)} %copy.40), channel_id=1, replica_groups=mesh['dom'=8,'feat'=4] {'feat'}, dimensions={1}, use_global_device_ids=true | all-gather | bytes 163840 | tf_op jit(solution)/shard_map/all_gather | solution.py:134
  219.1 0.9 fusion.30
  220.0 1.8 copy.35
  221.9 0.7 gather_fusion
  222.7 0.8 fusion.31
  (92 shorter events, 14.8 us)
Async XLA Ops:
  7.2 72.2 %copy-start = (bf16[256,256]{1,0:T(8,128)(2,1)S(1)}, bf16[256,256]{1,0:T(8,128)(2,1)}, u32[]{:S(2)}) copy-start(bf16[256,256]{1,0:T(8,128)(2,1)} %param.19) | copy-start | bytes 393220
  7.2 3.9 %copy-start.11 = (u32[32]{0:T(128)S(1)}, u32[32]{0:T(128)}, u32[]{:S(2)}) copy-start(u32[32]{0:T(128)} %constant.88) | copy-start | bytes 388
  7.2 5.1 %copy-start.10 = (s32[256]{0:T(256)S(1)}, s32[256]{0:T(256)}, u32[]{:S(2)}) copy-start(s32[256]{0:T(256)} %param.14) | copy-start | bytes 3076
  7.2 32.0 %copy-start.3 = (bf16[256,256]{1,0:T(8,128)(2,1)S(1)}, bf16[256,256]{1,0:T(8,128)(2,1)}, u32[]{:S(2)}) copy-start(bf16[256,256]{1,0:T(8,128)(2,1)} %param.18) | copy-start | bytes 393220
  7.2 32.0 %copy-start.4 = (bf16[256,256]{1,0:T(8,128)(2,1)S(1)}, bf16[256,256]{1,0:T(8,128)(2,1)}, u32[]{:S(2)}) copy-start(bf16[256,256]{1,0:T(8,128)(2,1)} %param.17) | copy-start | bytes 393220
  7.2 42.7 %reduce-scatter.3.cloned.1.call-start = ((), (), s32[]{:S(2)}) async-start(), calls=%async_computation.2 | async-start | bytes 1179648 | tf_op jit(solution)/shard_map/reduce_scatter | solution.py:62
  8.0 57.8 %copy-start.8 = (bf16[256,64]{0,1:T(8,128)(2,1)S(1)}, bf16[256,64]{0,1:T(8,128)(2,1)}, u32[]{:S(2)}) copy-start(bf16[256,64]{0,1:T(8,128)(2,1)} %param.13) | copy-start | bytes 98308
  10.9 69.3 %copy-start.9 = (bf16[256,64]{0,1:T(8,128)(2,1)S(1)}, bf16[256,64]{0,1:T(8,128)(2,1)}, u32[]{:S(2)}) copy-start(bf16[256,64]{0,1:T(8,128)(2,1)} %param.12) | copy-start | bytes 98308
  10.9 82.8 %copy-start.2 = (bf16[256,256]{1,0:T(8,128)(2,1)S(1)}, bf16[256,256]{1,0:T(8,128)(2,1)}, u32[]{:S(2)}) copy-start(bf16[256,256]{1,0:T(8,128)(2,1)} %param.16) | copy-start | bytes 393220
  11.0 83.2 %all-gather.3.cloned.1.call-start = ((), (), s32[]{:S(2)}) async-start(), calls=%async_computation.3 | async-start | bytes 1179648 | tf_op jit(solution)/shard_map/all_gather | solution.py:70
  65.7 108.6 %reduce-scatter.5.cloned.1.call-start = ((), (), s32[]{:S(2)}) async-start(), calls=%async_computation.4 | async-start | bytes 2359296 | tf_op jit(solution)/shard_map/reduce_scatter | solution.py:124
  98.3 1.2 copy-start.1
  99.5 0.8 copy-start.5
  106.0 1.2 copy-start.1
  107.2 0.8 copy-start.5
  124.5 67.2 %copy-start.6 = (bf16[4,64,64]{2,1,0:T(8,128)(2,1)S(1)}, bf16[4,64,64]{2,1,0:T(8,128)(2,1)}, u32[]{:S(2)}) copy-start(bf16[4,64,64]{2,1,0:T(8,128)(2,1)} %get-tuple-element.103) | copy-start | bytes 98308
  124.5 67.3 %copy-start.7 = (bf16[4,64,64]{2,1,0:T(8,128)(2,1)S(1)}, bf16[4,64,64]{2,1,0:T(8,128)(2,1)}, u32[]{:S(2)}) copy-start(bf16[4,64,64]{2,1,0:T(8,128)(2,1)} %get-tuple-element.102) | copy-start | bytes 98308
  124.5 95.5 %all-gather.5.cloned.1.call-start = ((), (), s32[]{:S(2)}) async-start(), calls=%async_computation.5 | async-start | bytes 1179648 | tf_op jit(solution)/shard_map/all_gather | solution.py:133
Sparse Core Ops, SparseCore 0:
  11.2 38.6 reduce-scatter.2
  65.8 23.9 all-gather.2
  124.6 49.6 reduce-scatter.4
  191.7 24.2 all-gather.4
where the time goes:
time: 231 us; the launch traced here: 230 us
  blocking collectives  109 us (47%)
  waiting for transfers between devices  59.1 us (26%)
  other arithmetic  15.7 us (7%)
  between operations  15.5 us (7%)
  local copies, waits for them, and re-layouts  15.4 us (7%)
  matrix products  12 us (5%)
  loops' own time  2.79 us (1%)
    reduce_scatter x1, waiting for transfers between devices, local(): lax.psum_scatter(kv_sum, 'dom', scatter_dimension=0, tiled=True)  48.4 us
    unnamed x1, blocking collectives  25.9 us
    all_gather x1, blocking collectives, local(): lax.all_gather(owned_grads, 'feat', axis=1, tiled=True)  15.4 us
    all_gather x1, blocking collectives, local(): lax.all_gather(attended, 'feat', axis=1, tiled=True)  13.9 us
    all_gather x1, blocking collectives, local(): owned_full = lax.all_gather(owned_cent, 'feat', axis=1, tiled=True)  13.8 us
    all_gather x1, blocking collectives, local(): grad_piece = lax.all_gather(cotangent, 'feat', axis=1, tiled=True)  13.5 us
    all_gather x1, blocking collectives, local(): x_piece = lax.all_gather(node_x, 'feat', axis=1, tiled=True)  13.5 us
    all_gather x1, blocking collectives, local(): lax.all_gather(g_query, 'feat', axis=1, tiled=True)  13.3 us
  transfers between devices with their start and end apart: 4, of which 2 were waited for; matrix products, arithmetic and copies ran while one was open for 2% of the time, Pallas kernels for 0%

commit v1 on v0

--- a/solution.py
+++ b/solution.py
@@ -1,10 +1,376 @@
+import functools
+
 import jax
 import jax.numpy as jnp
 from jax import lax
+from jax.experimental import pallas as pl
+from jax.experimental.pallas import tpu as pltpu
 from jax.sharding import PartitionSpec as P
 
 HEADS = 4
 CENTROIDS = 4096
+MESH = pl.DeviceIdType.MESH
+BF = jnp.bfloat16
+F32 = jnp.float32
+
+
+def dot(left, right, left_dim, right_dim):
+    return lax.dot_general(
+        left, right, (((left_dim,), (right_dim,)), ((), ())), preferred_element_type=F32
+    )
+
+
+def kernel(
+    n_dom,
+    n_feat,
+    x_ref,
+    cot_ref,
+    assign_ref,
+    size_ref,
+    wq_ref,
+    wk_ref,
+    wv_ref,
+    wo_ref,
+    out_ref,
+    gx_ref,
+    xp,
+    am,
+    xc,
+    ct,
+    rep,
+    kvb,
+    qg,
+    st,
+    gsend,
+    grecv,
+    aqs,
+    aqr,
+    kg,
+    aq,
+    e_buf,
+    g_buf,
+    xp_sem,
+    am_sem,
+    xc_sem,
+    ct_sem,
+    rep_sem,
+    kv_sem,
+    qg_sem,
+    st_sem,
+    gr_sem,
+    ap_sem,
+    kg_sem,
+    aq_sem,
+):
+    rows, width = x_ref.shape
+    half = rows // 2
+    n_plane = n_dom // 2
+    inv_root = 1.0 / width**0.5
+    dom = lax.axis_index("dom")
+    feat = lax.axis_index("feat")
+    core = lax.rem(dom, 2)
+    partner = dom + 1 - 2 * core
+
+    def dom_at(step):
+        return lax.rem(dom + step + n_dom, n_dom)
+
+    def feat_at(step):
+        return lax.rem(feat + step + n_feat, n_feat)
+
+    barrier = pltpu.get_barrier_semaphore()
+    for step in range(1, n_dom):
+        pl.semaphore_signal(
+            barrier, inc=1, device_id=(dom_at(step), feat), device_id_type=MESH
+        )
+    for step in range(1, n_feat):
+        pl.semaphore_signal(
+            barrier, inc=1, device_id=(dom, feat_at(step)), device_id_type=MESH
+        )
+
+    def send(src, dst, sems, slot, target):
+        copy = pltpu.make_async_remote_copy(
+            src_ref=src,
+            dst_ref=dst,
+            send_sem=sems.at[0, slot],
+            recv_sem=sems.at[1, slot],
+            device_id=target,
+            device_id_type=MESH,
+        )
+        copy.start()
+        return copy
+
+    size = size_ref[0]
+    lane_ids = lax.broadcasted_iota(jnp.int32, (1, rows), 1)
+    row_ids = lax.broadcasted_iota(jnp.int32, (rows, 1), 0)
+    alive = jnp.where(row_ids < size, 1.0, 0.0)
+    assign_row = assign_ref[...].astype(F32)
+    live_row = jnp.where(lane_ids < size, assign_row, -1.0)
+    x_own = x_ref[...]
+    xp[0] = jnp.concatenate([x_own[:half], x_own[half:]], axis=1)
+    am[0] = jnp.broadcast_to(live_row, (8, rows))
+    xc[feat] = jnp.concatenate([x_own, cot_ref[...]], axis=1)
+    pl.semaphore_wait(barrier, n_dom - 1 + n_feat - 1)
+
+    sent = []
+    xp_copies, am_copies = [None], [None]
+    for step in range(1, n_dom):
+        target = (dom_at(step), feat)
+        am_copies.append(send(am.at[0], am.at[step], am_sem, step, target))
+        xp_copies.append(send(xp.at[0], xp.at[step], xp_sem, step, target))
+    xc_copies = [None]
+    for step in range(1, n_feat):
+        xc_copies.append(
+            send(xc.at[feat], xc.at[feat], xc_sem, step, (dom, feat_at(step)))
+        )
+    sent += xp_copies[1:] + am_copies[1:] + xc_copies[1:]
+
+    def select(full):
+        out = full[:, :width]
+        for index in range(1, n_feat):
+            out = jnp.where(feat == index, full[:, index * width : (index + 1) * width], out)
+        return out
+
+    eye = row_ids == lane_ids
+    earlier = lane_ids < row_ids
+
+    def column(row):
+        return jnp.sum(jnp.where(eye, row, 0.0), axis=1, keepdims=True)
+
+    assign_col = column(assign_row)
+    counts = jnp.zeros((rows, 1), F32)
+    before = jnp.zeros((rows, 1), F32)
+    sums = jnp.zeros((rows, width), F32)
+    for step in range(n_dom):
+        if step:
+            am_copies[step].wait_recv()
+            xp_copies[step].wait_recv()
+        same = jnp.where(assign_col == am[step, 0:1, :], 1.0, 0.0)
+        block = jnp.sum(same, axis=1, keepdims=True)
+        counts = counts + block
+        if step:
+            before = before + block * jnp.where(step <= dom, 1.0, 0.0)
+        else:
+            before = jnp.sum(jnp.where(earlier, same, 0.0), axis=1, keepdims=True)
+        packed = xp[step]
+        piece = jnp.concatenate([packed[:, :width], packed[:, width:]], axis=0)
+        sums = sums + dot(same.astype(BF), piece, 1, 0)
+    inv_count = counts + 1.0
+    cent = (sums / inv_count).astype(BF)
+    ct[feat] = jnp.concatenate([cent[:half], cent[half:]], axis=1)
+    ct_copies = [None]
+    for step in range(1, n_feat):
+        ct_copies.append(
+            send(ct.at[feat], ct.at[feat], ct_sem, step, (dom, feat_at(step)))
+        )
+    rep_own = alive * jnp.where(before == 0.0, 1.0, 0.0)
+    rep_row = jnp.sum(jnp.where(eye, rep_own, 0.0), axis=0, keepdims=True)
+    rep[0] = jnp.broadcast_to(rep_row, (8, rows))
+    rep_copies = [None]
+    for step in range(1, n_dom):
+        rep_copies.append(
+            send(rep.at[0], rep.at[step], rep_sem, step, (dom_at(step), feat))
+        )
+    sent += ct_copies[1:] + rep_copies[1:]
+
+    for step in range(1, n_feat):
+        xc_copies[step].wait_recv()
+    x_full = jnp.concatenate([xc[index][:, :width] for index in range(n_feat)], axis=1)
+    cot_full = jnp.concatenate([xc[index][:, width:] for index in range(n_feat)], axis=1)
+    head_rows = pl.ds(pl.multiple_of(feat * width, width), width)
+    query = dot(x_full, select(wq_ref[...]), 1, 0).astype(BF)
+    g_att = (alive * dot(cot_full, wo_ref[head_rows, :], 1, 1)).astype(BF)
+    qg[0] = jnp.concatenate([query, g_att], axis=1)
+    qg_copy = send(qg.at[0], qg.at[1], qg_sem, 0, (partner, feat))
+    sent.append(qg_copy)
+
+    wkv = jnp.concatenate([select(wk_ref[...]), select(wv_ref[...])], axis=1)
+    wo_cols = select(wo_ref[...])
+    wq_rows = wq_ref[head_rows, :]
+    wk_rows = wk_ref[head_rows, :]
+    wv_rows = wv_ref[head_rows, :]
+
+    empty = jnp.full((1, 1), float(CENTROIDS), F32)
+    for step in range(n_dom):
+        if step:
+            rep_copies[step].wait_recv()
+        empty = empty - jnp.sum(rep[step, 0:1, :], axis=1, keepdims=True)
+    rep_cols = [rep_own] + [column(rep[2 * step, 0:1, :]) for step in range(1, n_plane)]
+
+    for step in range(1, n_feat):
+        ct_copies[step].wait_recv()
+    cent_full = jnp.concatenate(
+        [
+            jnp.concatenate([ct[index][:, :width], ct[index][:, width:]], axis=0)
+            for index in range(n_feat)
+        ],
+        axis=1,
+    )
+    kvb[0] = dot(cent_full, wkv, 1, 0).astype(BF)
+    kv_copies = [None]
+    for step in range(1, n_plane):
+        kv_copies.append(
+            send(kvb.at[0], kvb.at[step], kv_sem, step, (dom_at(2 * step), feat))
+        )
+    sent += kv_copies[1:]
+
+    qg_copy.wait_recv()
+    low_lane = lax.broadcasted_iota(jnp.int32, (1, 2 * width), 1) < width
+    qg_all = jnp.concatenate([qg[0], qg[1]], axis=0).astype(F32)
+    q_low = jnp.where(low_lane, qg_all, 0.0).astype(BF)
+    g_high = jnp.where(low_lane, 0.0, qg_all).astype(BF)
+
+    tops, zs, ds = [], [], []
+    for step in range(n_plane):
+        if step:
+            kv_copies[step].wait_recv()
+        kv = kvb[step]
+        scores = dot(kv, q_low, 1, 1) * inv_root
+        g_probs = dot(kv, g_high, 1, 1)
+        top = jnp.maximum(jnp.max(scores, axis=0, keepdims=True), 0.0)
+        expo = jnp.exp(scores - top)
+        e_buf[step] = expo
+        g_buf[step] = g_probs
+        counted = expo * rep_cols[step]
+        tops.append(top)
+        zs.append(jnp.sum(counted, axis=0, keepdims=True))
+        ds.append(jnp.sum(counted * g_probs, axis=0, keepdims=True))
+    top = functools.reduce(jnp.maximum, tops)
+    fix = [jnp.exp(one - top) for one in tops]
+    z_own = sum(one * scale for one, scale in zip(zs, fix))
+    d_own = sum(one * scale for one, scale in zip(ds, fix))
+    st[0, 0:1, :] = top
+    st[0, 1:2, :] = z_own
+    st[0, 2:3, :] = d_own
+    st[0, 3:8, :] = jnp.zeros((5, 2 * rows), F32)
+    st_copy = send(st.at[0], st.at[1], st_sem, 0, (partner, feat))
+    sent.append(st_copy)
+    st_copy.wait_recv()
+    other = st[1]
+    other = jnp.concatenate([other[:, rows:], other[:, :rows]], axis=1)
+    top_all = jnp.maximum(top, other[0:1])
+    own_fix = jnp.exp(top - top_all)
+    other_fix = jnp.exp(other[0:1] - top_all)
+    z_all = z_own * own_fix + other[1:2] * other_fix + empty * jnp.exp(-top_all)
+    delta = (d_own * own_fix + other[2:3] * other_fix) / z_all
+
+    totals = jnp.zeros((2 * width, 2 * rows), F32)
+    gr_copies = [None] * n_plane
+    kv_own = None
+    for step in list(range(1, n_plane)) + [0]:
+        scale = jnp.exp(tops[step] - top_all) / z_all
+        probs = e_buf[step] * scale
+        probs_low = probs.astype(BF)
+        g_scores = (probs * (g_buf[step] - delta) * inv_root).astype(BF)
+        partial = dot(g_scores, q_low, 1, 0) + dot(probs_low, g_high, 1, 0)
+        if step:
+            gsend[step] = partial.astype(BF)
+            gr_copies[step] = send(
+                gsend.at[step], grecv.at[step], gr_sem, step, (dom_at(-2 * step), feat)
+            )
+        else:
+            kv_own = partial
+        kv = kvb[step].astype(F32) * rep_cols[step]
+        k_low = jnp.where(low_lane, kv, 0.0).astype(BF)
+        v_high = jnp.where(low_lane, 0.0, kv).astype(BF)
+        totals = totals + dot(k_low, g_scores, 0, 0) + dot(v_high, probs_low, 0, 0)
+    sent += gr_copies[1:]
+    aqs[...] = totals[:, rows:]
+    ap_copy = send(aqs, aqr, ap_sem, 0, (partner, feat))
+    sent.append(ap_copy)
+    ap_copy.wait_recv()
+    aq[feat] = (totals[:, :rows] + aqr[...]).astype(BF)
+    aq_copies = [None]
+    for step in range(1, n_feat):
+        aq_copies.append(
+            send(aq.at[feat], aq.at[feat], aq_sem, step, (dom, feat_at(step)))
+        )
+    for step in range(1, n_plane):
+        gr_copies[step].wait_recv()
+        kv_own = kv_own + grecv[step].astype(F32)
+    kg[feat] = kv_own.astype(BF)
+    kg_copies = [None]
+    for step in range(1, n_feat):
+        kg_copies.append(
+            send(kg.at[feat], kg.at[feat], kg_sem, step, (dom, feat_at(step)))
+        )
+    sent += aq_copies[1:] + kg_copies[1:]
+    for step in range(1, n_feat):
+        aq_copies[step].wait_recv()
+    gq_full = jnp.concatenate([aq[index][:width] for index in range(n_feat)], axis=0)
+    att_full = jnp.concatenate([aq[index][width:] for index in range(n_feat)], axis=0)
+    out_ref[...] = (alive * dot(att_full, wo_cols, 0, 0)).astype(BF)
+    grad = dot(gq_full, wq_rows, 0, 1)
+    for step in range(1, n_feat):
+        kg_copies[step].wait_recv()
+    cent_grad = jnp.zeros((rows, width), F32)
+    for index in range(n_feat):
+        spot = slice(index * width, (index + 1) * width)
+        stacked = jnp.concatenate([wk_rows[:, spot], wv_rows[:, spot]], axis=1)
+        cent_grad = cent_grad + dot(kg[index], stacked, 1, 1)
+    gx_ref[...] = (grad + alive * (cent_grad / inv_count)).astype(BF)
+    for copy in sent:
+        copy.wait_send()
+
+
+def fused(n_dom, n_feat, node_x, cotangent, assign, part_sizes, w_query, w_key, w_value, w_out):
+    rows, width = node_x.shape
+    n_plane = n_dom // 2
+    vmem = pl.BlockSpec(memory_space=pltpu.VMEM)
+    smem = pl.BlockSpec(memory_space=pltpu.SMEM)
+    pair = 2 * width
+
+    def sems(count):
+        return pltpu.SemaphoreType.DMA((2, count))
+
+    return pl.pallas_call(
+        functools.partial(kernel, n_dom, n_feat),
+        out_shape=(
+            jax.ShapeDtypeStruct((rows, width), BF),
+            jax.ShapeDtypeStruct((rows, width), BF),
+        ),
+        in_specs=[vmem, vmem, vmem, smem, vmem, vmem, vmem, vmem],
+        out_specs=(vmem, vmem),
+        scratch_shapes=[
+            pltpu.VMEM((n_dom, rows // 2, pair), BF),
+            pltpu.VMEM((n_dom, 8, rows), F32),
+            pltpu.VMEM((n_feat, rows, pair), BF),
+            pltpu.VMEM((n_feat, rows // 2, pair), BF),
+            pltpu.VMEM((n_dom, 8, rows), F32),
+            pltpu.VMEM((n_plane, rows, pair), BF),
+            pltpu.VMEM((2, rows, pair), BF),
+            pltpu.VMEM((2, 8, 2 * rows), F32),
+            pltpu.VMEM((n_plane, rows, pair), BF),
+            pltpu.VMEM((n_plane, rows, pair), BF),
+            pltpu.VMEM((pair, rows), F32),
+            pltpu.VMEM((pair, rows), F32),
+            pltpu.VMEM((n_feat, rows, pair), BF),
+            pltpu.VMEM((n_feat, pair, rows), BF),
+            pltpu.VMEM((n_plane, rows, 2 * rows), F32),
+            pltpu.VMEM((n_plane, rows, 2 * rows), F32),
+            sems(n_dom),
+            sems(n_dom),
+            sems(n_feat),
+            sems(n_feat),
+            sems(n_dom),
+            sems(n_plane),
+            sems(1),
+            sems(1),
+            sems(n_plane),
+            sems(1),
+            sems(n_feat),
+            sems(n_feat),
+        ],
+        compiler_params=pltpu.CompilerParams(collective_id=0, has_side_effects=True),
+    )(
+        node_x,
+        cotangent,
+        assign.reshape(1, rows),
+        part_sizes,
+        w_query,
+        w_key,
+        w_value,
+        w_out,
+    )
 
 
 def trans_dot(left, right):
@@ -138,8 +504,15 @@
 
 def solution(mesh):
     placed = (P("dom", "feat"), P("dom", "feat"), P("dom"), P("dom"), P(), P(), P(), P())
+    n_dom, n_feat = mesh.shape["dom"], mesh.shape["feat"]
+
+    def step(node_x, *rest):
+        if n_dom % 2 == 0 and n_dom * node_x.shape[0] < CENTROIDS:
+            return fused(n_dom, n_feat, node_x, *rest)
+        return local(node_x, *rest)
+
     return jax.shard_map(
-        local,
+        step,
         mesh=mesh,
         in_specs=placed,
         out_specs=(P("dom", "feat"), P("dom", "feat")),

time: 231 us -> 47.1 us (0.20)
  blocking collectives: 109 us -> 0 us
  waiting for transfers between devices: 59.1 us -> 0 us
  Pallas kernels: 0 us -> 41 us
  other arithmetic: 15.7 us -> 0 us
  between operations: 15.5 us -> 1.3 us
  matrix products: 12 us -> 0 us
  local copies, waits for them, and re-layouts: 15.4 us -> 4.51 us
  loops' own time: 2.79 us -> 0 us
    all_gather x6 -> x0, blocking collectives: 83.6 us -> none  [the longest x1 15.4 us: local(): lax.all_gather(owned_grads, 'feat', axis=1, tiled=True)]
    reduce_scatter x2 -> x0, waiting for transfers between devices: 59 us -> none  [the longest x1 48.4 us: local(): lax.psum_scatter(kv_sum, 'dom', scatter_dimension=0, tiled=True)]
    pallas_call x0 -> x1, Pallas kernels: none -> 41 us  [fused(): pl.pallas_call(functools.partial(kernel, n_dom, n_feat), out_shape=(jax.S...]
    unnamed x1 -> x0, blocking collectives: 25.9 us -> none
    dot_general x19 -> x0, matrix products: 12 us -> none  [the longest x5 4.35 us: inner_dot(): lax.dot_general(left, right, (((0,), (0,)), ((), ())), preferred_element_...]
    add x5 -> x0, other arithmetic: 11.1 us -> none  [the longest x4 11 us: step_block(): return (running + kv_part, (attended, g_query))]
    dynamic_slice x6 -> x0, local copies, waits for them, and re-layouts: 3.33 us -> none  [the longest x4 2.44 us: local(): lax.scan(step_block, start_grads, (query.reshape(4, quarter, head_width),...]
    slice x1 -> x0, local copies, waits for them, and re-layouts: 2.9 us -> none  [local(): values = key_value[:, head_width:]]
  transfers between devices with their start and end apart: 4 -> 0, of which waited for: 2 -> 0; matrix products, arithmetic and copies ran while one was open for 2% -> 0% of each run, Pallas kernels for 0% -> 0%
where the time goes in v1:
time: 47.1 us; the launch traced here: 46.8 us
  Pallas kernels  41 us (87%)
  local copies, waits for them, and re-layouts  4.51 us (10%)
  between operations  1.3 us (3%)
    pallas_call x1, Pallas kernels, fused(): pl.pallas_call(functools.partial(kernel, n_dom, n_feat), out_shape=(jax.S...  41 us
    pallas_call x2, local copies, waits for them, and re-layouts, fused(): pl.pallas_call(functools.partial(kernel, n_dom, n_feat), out_shape=(jax.S...  2.28 us
    unnamed x6, local copies, waits for them, and re-layouts  2.22 us

profile of v1, /device:TPU:0, one launch (start us, length us, event | category | flops | bytes accessed | tf_op | source)
XLA Modules:
  0.0 46.8 jit_solution(826528216159918963)
XLA Ops:
  1.3 0.0 copy-start.1
  1.3 1.5 %copy.10.x_ref = bf16[256,64]{1,0:T(8,128)(2,1)} copy(bf16[256,64]{0,1:T(8,128)(2,1)} %param.8) | data formatting | bytes 65536 | tf_op args[0]
  2.8 0.0 copy-done.1
  2.8 0.7 %copy.11.cot_ref = bf16[256,64]{1,0:T(8,128)(2,1)} copy(bf16[256,64]{0,1:T(8,128)(2,1)S(1)} %copy-done.1) | data formatting | bytes 65536 | tf_op args[1]
  3.5 41.0 %shard_map.95 = (bf16[256,64]{1,0:T(8,128)(2,1)}, bf16[256,64]{1,0:T(8,128)(2,1)}) custom-call(bf16[256,64]{1,0:T(8,128)(2,1)} %copy.10.x_ref, bf16[256,64]{1,0:T(8,128)(2,1)} %copy.11.cot_ref, s32[1,256]{1,0:T(1,128)} %bitcast.1, s32[1]{0:T(128)S(6)} %copy.14.size_ref, bf16[256,256]{1,0:T(8,128)(2,1)} %wq_ref.1, bf16[256,256]{1,0:T(8,128)(2,1)} %wk_ref.1, ...), custom_call_target="tpu_custom_call" | custom-call | tf_op jit(solution)/shard_map/pallas_call | solution.py:325
  44.5 0.0 copy-start
  44.6 1.6 %copy.12 = bf16[256,64]{0,1:T(8,128)(2,1)} copy(bf16[256,64]{1,0:T(8,128)(2,1)} %get-tuple-element.2) | data formatting | bytes 65536 | tf_op jit(solution)/shard_map/pallas_call | solution.py:325
  46.1 0.0 copy-done
  46.1 0.7 %copy.13 = bf16[256,64]{0,1:T(8,128)(2,1)} copy(bf16[256,64]{1,0:T(8,128)(2,1)S(1)} %copy-done) | data formatting | bytes 65536 | tf_op jit(solution)/shard_map/pallas_call | solution.py:325
Async XLA Ops:
  1.3 1.5 %copy-start.1 = (bf16[256,64]{0,1:T(8,128)(2,1)S(1)}, bf16[256,64]{0,1:T(8,128)(2,1)}, u32[]{:S(2)}) copy-start(bf16[256,64]{0,1:T(8,128)(2,1)} %param.9) | copy-start | bytes 98308
  44.5 1.6 %copy-start = (bf16[256,64]{1,0:T(8,128)(2,1)S(1)}, bf16[256,64]{1,0:T(8,128)(2,1)}, u32[]{:S(2)}) copy-start(bf16[256,64]{1,0:T(8,128)(2,1)} %get-tuple-element.3) | copy-start | bytes 98308

commit v2 on v1

--- a/solution.py
+++ b/solution.py
@@ -62,8 +62,7 @@
     kg_sem,
     aq_sem,
 ):
-    rows, width = x_ref.shape
-    half = rows // 2
+    width, rows = x_ref.shape
     n_plane = n_dom // 2
     inv_root = 1.0 / width**0.5
     dom = lax.axis_index("dom")
@@ -102,13 +101,12 @@
     size = size_ref[0]
     lane_ids = lax.broadcasted_iota(jnp.int32, (1, rows), 1)
     row_ids = lax.broadcasted_iota(jnp.int32, (rows, 1), 0)
-    alive = jnp.where(row_ids < size, 1.0, 0.0)
+    alive = jnp.where(lane_ids < size, 1.0, 0.0)
     assign_row = assign_ref[...].astype(F32)
-    live_row = jnp.where(lane_ids < size, assign_row, -1.0)
-    x_own = x_ref[...]
-    xp[0] = jnp.concatenate([x_own[:half], x_own[half:]], axis=1)
-    am[0] = jnp.broadcast_to(live_row, (8, rows))
-    xc[feat] = jnp.concatenate([x_own, cot_ref[...]], axis=1)
+    am[0] = jnp.broadcast_to(jnp.where(lane_ids < size, assign_row, -1.0), (8, rows))
+    xp[0] = x_ref[...]
+    xc[feat, :width] = x_ref[...]
+    xc[feat, width:] = cot_ref[...]
     pl.semaphore_wait(barrier, n_dom - 1 + n_feat - 1)
 
     sent = []
@@ -130,6 +128,15 @@
             out = jnp.where(feat == index, full[:, index * width : (index + 1) * width], out)
         return out
 
+    head_rows = pl.ds(pl.multiple_of(feat * width, width), width)
+    wkv = jnp.concatenate([select(wk_ref[...]), select(wv_ref[...])], axis=1)
+    wq_cols = select(wq_ref[...])
+    wo_cols = select(wo_ref[...])
+    wq_rows = wq_ref[head_rows, :]
+    wk_rows = wk_ref[head_rows, :]
+    wv_rows = wv_ref[head_rows, :]
+    wo_rows = wo_ref[head_rows, :]
+
     eye = row_ids == lane_ids
     earlier = lane_ids < row_ids
 
@@ -137,34 +144,32 @@
         return jnp.sum(jnp.where(eye, row, 0.0), axis=1, keepdims=True)
 
     assign_col = column(assign_row)
-    counts = jnp.zeros((rows, 1), F32)
-    before = jnp.zeros((rows, 1), F32)
-    sums = jnp.zeros((rows, width), F32)
+    mark_ids = lax.broadcasted_iota(jnp.int32, (16, rows), 0)
+    sums = jnp.zeros((width + 16, rows), F32)
+    before = jnp.zeros((1, rows), F32)
     for step in range(n_dom):
         if step:
             am_copies[step].wait_recv()
+        same = jnp.where(assign_col == am[step, 0:1, :], 1.0, 0.0)
+        first = jnp.where(step <= dom, 1.0, 0.0) if step else 0.0
+        marks = jnp.where(mark_ids == 0, 1.0, jnp.where(mark_ids == 1, first, 0.0))
+        if step:
             xp_copies[step].wait_recv()
-        same = jnp.where(assign_col == am[step, 0:1, :], 1.0, 0.0)
-        block = jnp.sum(same, axis=1, keepdims=True)
-        counts = counts + block
-        if step:
-            before = before + block * jnp.where(step <= dom, 1.0, 0.0)
         else:
-            before = jnp.sum(jnp.where(earlier, same, 0.0), axis=1, keepdims=True)
-        packed = xp[step]
-        piece = jnp.concatenate([packed[:, :width], packed[:, width:]], axis=0)
-        sums = sums + dot(same.astype(BF), piece, 1, 0)
-    inv_count = counts + 1.0
-    cent = (sums / inv_count).astype(BF)
-    ct[feat] = jnp.concatenate([cent[:half], cent[half:]], axis=1)
+            lower = jnp.where(earlier, same, 0.0).astype(BF)
+            before = dot(jnp.ones((16, rows), BF), lower, 1, 1)[0:1]
+        piece = jnp.concatenate([xp[step], marks.astype(BF)], axis=0)
+        sums = sums + dot(piece, same.astype(BF), 1, 1)
+    inv_count = sums[width : width + 1] + 1.0
+    before = before + sums[width + 1 : width + 2]
+    ct[feat] = (sums[:width] / inv_count).astype(BF)
     ct_copies = [None]
     for step in range(1, n_feat):
         ct_copies.append(
             send(ct.at[feat], ct.at[feat], ct_sem, step, (dom, feat_at(step)))
         )
     rep_own = alive * jnp.where(before == 0.0, 1.0, 0.0)
-    rep_row = jnp.sum(jnp.where(eye, rep_own, 0.0), axis=0, keepdims=True)
-    rep[0] = jnp.broadcast_to(rep_row, (8, rows))
+    rep[0] = jnp.broadcast_to(rep_own, (8, rows))
     rep_copies = [None]
     for step in range(1, n_dom):
         rep_copies.append(
@@ -174,58 +179,47 @@
 
     for step in range(1, n_feat):
         xc_copies[step].wait_recv()
-    x_full = jnp.concatenate([xc[index][:, :width] for index in range(n_feat)], axis=1)
-    cot_full = jnp.concatenate([xc[index][:, width:] for index in range(n_feat)], axis=1)
-    head_rows = pl.ds(pl.multiple_of(feat * width, width), width)
-    query = dot(x_full, select(wq_ref[...]), 1, 0).astype(BF)
-    g_att = (alive * dot(cot_full, wo_ref[head_rows, :], 1, 1)).astype(BF)
-    qg[0] = jnp.concatenate([query, g_att], axis=1)
+    x_full = jnp.concatenate([xc[index][:width] for index in range(n_feat)], axis=0)
+    cot_full = jnp.concatenate([xc[index][width:] for index in range(n_feat)], axis=0)
+    qg[0, :width] = dot(wq_cols, x_full, 0, 0).astype(BF)
+    qg[0, width:] = (alive * dot(wo_rows, cot_full, 1, 0)).astype(BF)
     qg_copy = send(qg.at[0], qg.at[1], qg_sem, 0, (partner, feat))
     sent.append(qg_copy)
-
-    wkv = jnp.concatenate([select(wk_ref[...]), select(wv_ref[...])], axis=1)
-    wo_cols = select(wo_ref[...])
-    wq_rows = wq_ref[head_rows, :]
-    wk_rows = wk_ref[head_rows, :]
-    wv_rows = wv_ref[head_rows, :]
 
     empty = jnp.full((1, 1), float(CENTROIDS), F32)
     for step in range(n_dom):
         if step:
             rep_copies[step].wait_recv()
         empty = empty - jnp.sum(rep[step, 0:1, :], axis=1, keepdims=True)
-    rep_cols = [rep_own] + [column(rep[2 * step, 0:1, :]) for step in range(1, n_plane)]
+    rep_cols = [column(rep[2 * step, 0:1, :]) for step in range(n_plane)]
+
+    qg_copy.wait_recv()
+    qg_all = jnp.concatenate([qg[0], qg[1]], axis=1)
+    blank = jnp.zeros((width, 2 * rows), BF)
+    q_rows = jnp.concatenate([qg_all[:width], blank], axis=0)
+    g_rows = jnp.concatenate([blank, qg_all[width:]], axis=0)
+    q_low = q_rows.T
+    g_high = g_rows.T
+    low_lane = lax.broadcasted_iota(jnp.int32, (1, 2 * width), 1) < width
 
     for step in range(1, n_feat):
         ct_copies[step].wait_recv()
-    cent_full = jnp.concatenate(
-        [
-            jnp.concatenate([ct[index][:, :width], ct[index][:, width:]], axis=0)
-            for index in range(n_feat)
-        ],
-        axis=1,
-    )
-    kvb[0] = dot(cent_full, wkv, 1, 0).astype(BF)
+    cent_full = ct[...].reshape(n_feat * width, rows)
+    kvb[0] = dot(cent_full, wkv, 0, 0).astype(BF)
     kv_copies = [None]
     for step in range(1, n_plane):
         kv_copies.append(
             send(kvb.at[0], kvb.at[step], kv_sem, step, (dom_at(2 * step), feat))
         )
     sent += kv_copies[1:]
-
-    qg_copy.wait_recv()
-    low_lane = lax.broadcasted_iota(jnp.int32, (1, 2 * width), 1) < width
-    qg_all = jnp.concatenate([qg[0], qg[1]], axis=0).astype(F32)
-    q_low = jnp.where(low_lane, qg_all, 0.0).astype(BF)
-    g_high = jnp.where(low_lane, 0.0, qg_all).astype(BF)
 
     tops, zs, ds = [], [], []
     for step in range(n_plane):
         if step:
             kv_copies[step].wait_recv()
         kv = kvb[step]
-        scores = dot(kv, q_low, 1, 1) * inv_root
-        g_probs = dot(kv, g_high, 1, 1)
+        scores = dot(kv, q_rows, 1, 0) * inv_root
+        g_probs = dot(kv, g_rows, 1, 0)
         top = jnp.maximum(jnp.max(scores, axis=0, keepdims=True), 0.0)
         expo = jnp.exp(scores - top)
         e_buf[step] = expo
@@ -298,15 +292,15 @@
         aq_copies[step].wait_recv()
     gq_full = jnp.concatenate([aq[index][:width] for index in range(n_feat)], axis=0)
     att_full = jnp.concatenate([aq[index][width:] for index in range(n_feat)], axis=0)
-    out_ref[...] = (alive * dot(att_full, wo_cols, 0, 0)).astype(BF)
-    grad = dot(gq_full, wq_rows, 0, 1)
+    out_ref[...] = (alive * dot(wo_cols, att_full, 0, 0)).astype(BF)
+    grad = dot(wq_rows, gq_full, 1, 0)
     for step in range(1, n_feat):
         kg_copies[step].wait_recv()
-    cent_grad = jnp.zeros((rows, width), F32)
+    cent_grad = jnp.zeros((width, rows), F32)
     for index in range(n_feat):
         spot = slice(index * width, (index + 1) * width)
         stacked = jnp.concatenate([wk_rows[:, spot], wv_rows[:, spot]], axis=1)
-        cent_grad = cent_grad + dot(kg[index], stacked, 1, 1)
+        cent_grad = cent_grad + dot(stacked, kg[index], 1, 1)
     gx_ref[...] = (grad + alive * (cent_grad / inv_count)).astype(BF)
     for copy in sent:
         copy.wait_send()
@@ -322,22 +316,22 @@
     def sems(count):
         return pltpu.SemaphoreType.DMA((2, count))
 
-    return pl.pallas_call(
+    out, grad = pl.pallas_call(
         functools.partial(kernel, n_dom, n_feat),
         out_shape=(
-            jax.ShapeDtypeStruct((rows, width), BF),
-            jax.ShapeDtypeStruct((rows, width), BF),
+            jax.ShapeDtypeStruct((width, rows), BF),
+            jax.ShapeDtypeStruct((width, rows), BF),
         ),
         in_specs=[vmem, vmem, vmem, smem, vmem, vmem, vmem, vmem],
         out_specs=(vmem, vmem),
         scratch_shapes=[
-            pltpu.VMEM((n_dom, rows // 2, pair), BF),
+            pltpu.VMEM((n_dom, width, rows), BF),
             pltpu.VMEM((n_dom, 8, rows), F32),
-            pltpu.VMEM((n_feat, rows, pair), BF),
-            pltpu.VMEM((n_feat, rows // 2, pair), BF),
+            pltpu.VMEM((n_feat, pair, rows), BF),
+            pltpu.VMEM((n_feat, width, rows), BF),
             pltpu.VMEM((n_dom, 8, rows), F32),
             pltpu.VMEM((n_plane, rows, pair), BF),
-            pltpu.VMEM((2, rows, pair), BF),
+            pltpu.VMEM((2, pair, rows), BF),
             pltpu.VMEM((2, 8, 2 * rows), F32),
             pltpu.VMEM((n_plane, rows, pair), BF),
             pltpu.VMEM((n_plane, rows, pair), BF),
@@ -362,8 +356,8 @@
         ],
         compiler_params=pltpu.CompilerParams(collective_id=0, has_side_effects=True),
     )(
-        node_x,
-        cotangent,
+        node_x.T,
+        cotangent.T,
         assign.reshape(1, rows),
         part_sizes,
         w_query,
@@ -371,6 +365,7 @@
         w_value,
         w_out,
     )
+    return out.T, grad.T
 
 
 def trans_dot(left, right):

time: 47.1 us -> 44 us (0.934)
  local copies, waits for them, and re-layouts: 4.51 us -> 2 us
  Pallas kernels: 41 us -> 40.5 us
    pallas_call x2 -> x0, local copies, waits for them, and re-layouts: 2.28 us -> none  [fused(): pl.pallas_call(functools.partial(kernel, n_dom, n_feat), out_shape=(jax.S...]
    pallas_call x1, Pallas kernels: 41 us -> 40.5 us  [fused(): pl.pallas_call(functools.partial(kernel, n_dom, n_feat), out_shape=(jax.S...]
    unnamed x6 -> x4, local copies, waits for them, and re-layouts: 2.22 us -> 2 us
where the time goes in v2:
time: 44 us; the launch traced here: 43.8 us
  Pallas kernels  40.5 us (92%)
  local copies, waits for them, and re-layouts  2 us (5%)
  between operations  1.29 us (3%)
    pallas_call x1, Pallas kernels, fused(): pl.pallas_call(functools.partial(kernel, n_dom, n_feat), out_shape=(jax.S...  40.5 us
    unnamed x4, local copies, waits for them, and re-layouts  2 us

profile of v2, /device:TPU:0, one launch (start us, length us, event | category | flops | bytes accessed | tf_op | source)
XLA Modules:
  0.0 43.8 jit_solution(1729616688800654960)
XLA Ops:
  1.3 40.5 %shard_map.95 = (bf16[64,256]{1,0:T(8,128)(2,1)}, bf16[64,256]{1,0:T(8,128)(2,1)}) custom-call(bf16[64,256]{1,0:T(8,128)(2,1)} %bitcast.7, bf16[64,256]{1,0:T(8,128)(2,1)} %bitcast.8, s32[1,256]{1,0:T(1,128)} %bitcast.9, s32[1]{0:T(128)S(6)} %copy.12.size_ref, bf16[256,256]{1,0:T(8,128)(2,1)} %wq_ref.1, bf16[256,256]{1,0:T(8,128)(2,1)} %wk_ref.1, ...), custom_call_target="tpu_custom_call" | custom-call | tf_op jit(solution)/shard_map/pallas_call | solution.py:319
  41.8 0.0 copy-start
  41.8 1.4 %copy.13 = bf16[256,64]{0,1:T(8,128)(2,1)} copy(bf16[256,64]{0,1:T(8,128)(2,1)} %bitcast.6) | data formatting | bytes 65536
  43.2 0.0 copy-done
  43.2 0.6 %copy.14 = bf16[256,64]{0,1:T(8,128)(2,1)} copy(bf16[256,64]{0,1:T(8,128)(2,1)S(1)} %bitcast.5) | data formatting | bytes 65536
Async XLA Ops:
  41.8 1.4 %copy-start = (bf16[64,256]{1,0:T(8,128)(2,1)S(1)}, bf16[64,256]{1,0:T(8,128)(2,1)}, u32[]{:S(2)}) copy-start(bf16[64,256]{1,0:T(8,128)(2,1)} %get-tuple-element.5) | copy-start | bytes 98308

commit v3 on v2

--- a/solution.py
+++ b/solution.py
@@ -45,8 +45,11 @@
     grecv,
     aqs,
     aqr,
-    kg,
+    xg,
     aq,
+    part,
+    gp,
+    gpr,
     e_buf,
     g_buf,
     xp_sem,
@@ -59,8 +62,9 @@
     st_sem,
     gr_sem,
     ap_sem,
-    kg_sem,
+    gp_sem,
     aq_sem,
+    co_sem,
 ):
     width, rows = x_ref.shape
     n_plane = n_dom // 2
@@ -105,22 +109,8 @@
     assign_row = assign_ref[...].astype(F32)
     am[0] = jnp.broadcast_to(jnp.where(lane_ids < size, assign_row, -1.0), (8, rows))
     xp[0] = x_ref[...]
-    xc[feat, :width] = x_ref[...]
-    xc[feat, width:] = cot_ref[...]
-    pl.semaphore_wait(barrier, n_dom - 1 + n_feat - 1)
-
-    sent = []
-    xp_copies, am_copies = [None], [None]
-    for step in range(1, n_dom):
-        target = (dom_at(step), feat)
-        am_copies.append(send(am.at[0], am.at[step], am_sem, step, target))
-        xp_copies.append(send(xp.at[0], xp.at[step], xp_sem, step, target))
-    xc_copies = [None]
-    for step in range(1, n_feat):
-        xc_copies.append(
-            send(xc.at[feat], xc.at[feat], xc_sem, step, (dom, feat_at(step)))
-        )
-    sent += xp_copies[1:] + am_copies[1:] + xc_copies[1:]
+    xg[feat] = x_ref[...]
+    xc[feat] = cot_ref[...]
 
     def select(full):
         out = full[:, :width]
@@ -132,9 +122,6 @@
     wkv = jnp.concatenate([select(wk_ref[...]), select(wv_ref[...])], axis=1)
     wq_cols = select(wq_ref[...])
     wo_cols = select(wo_ref[...])
-    wq_rows = wq_ref[head_rows, :]
-    wk_rows = wk_ref[head_rows, :]
-    wv_rows = wv_ref[head_rows, :]
     wo_rows = wo_ref[head_rows, :]
 
     eye = row_ids == lane_ids
@@ -145,21 +132,35 @@
 
     assign_col = column(assign_row)
     mark_ids = lax.broadcasted_iota(jnp.int32, (16, rows), 0)
-    sums = jnp.zeros((width + 16, rows), F32)
-    before = jnp.zeros((1, rows), F32)
-    for step in range(n_dom):
-        if step:
-            am_copies[step].wait_recv()
+
+    def add_block(step, sums):
         same = jnp.where(assign_col == am[step, 0:1, :], 1.0, 0.0)
         first = jnp.where(step <= dom, 1.0, 0.0) if step else 0.0
         marks = jnp.where(mark_ids == 0, 1.0, jnp.where(mark_ids == 1, first, 0.0))
-        if step:
-            xp_copies[step].wait_recv()
-        else:
-            lower = jnp.where(earlier, same, 0.0).astype(BF)
-            before = dot(jnp.ones((16, rows), BF), lower, 1, 1)[0:1]
         piece = jnp.concatenate([xp[step], marks.astype(BF)], axis=0)
-        sums = sums + dot(piece, same.astype(BF), 1, 1)
+        return sums + dot(piece, same.astype(BF), 1, 1)
+
+    own_live = jnp.where(lane_ids < size, assign_row, -1.0)
+    lower = jnp.where(earlier & (assign_col == own_live), 1.0, 0.0).astype(BF)
+    before = dot(jnp.ones((16, rows), BF), lower, 1, 1)[0:1]
+    sums = add_block(0, jnp.zeros((width + 16, rows), F32))
+
+    pl.semaphore_wait(barrier, n_dom - 1 + n_feat - 1)
+    sent = []
+    xp_copies, am_copies, xg_copies = [None], [None], [None]
+    for step in range(1, n_dom):
+        target = (dom_at(step), feat)
+        am_copies.append(send(am.at[0], am.at[step], am_sem, step, target))
+        xp_copies.append(send(xp.at[0], xp.at[step], xp_sem, step, target))
+    for step in range(1, n_feat):
+        xg_copies.append(
+            send(xg.at[feat], xg.at[feat], xc_sem, step, (dom, feat_at(step)))
+        )
+    sent += xp_copies[1:] + am_copies[1:] + xg_copies[1:]
+    for step in range(1, n_dom):
+        am_copies[step].wait_recv()
+        xp_copies[step].wait_recv()
+        sums = add_block(step, sums)
     inv_count = sums[width : width + 1] + 1.0
     before = before + sums[width + 1 : width + 2]
     ct[feat] = (sums[:width] / inv_count).astype(BF)
@@ -167,6 +168,11 @@
     for step in range(1, n_feat):
         ct_copies.append(
             send(ct.at[feat], ct.at[feat], ct_sem, step, (dom, feat_at(step)))
+        )
+    xc_copies = [None]
+    for step in range(1, n_feat):
+        xc_copies.append(
+            send(xc.at[feat], xc.at[feat], co_sem, step, (dom, feat_at(step)))
         )
     rep_own = alive * jnp.where(before == 0.0, 1.0, 0.0)
     rep[0] = jnp.broadcast_to(rep_own, (8, rows))
@@ -175,16 +181,11 @@
         rep_copies.append(
             send(rep.at[0], rep.at[step], rep_sem, step, (dom_at(step), feat))
         )
-    sent += ct_copies[1:] + rep_copies[1:]
-
-    for step in range(1, n_feat):
-        xc_copies[step].wait_recv()
-    x_full = jnp.concatenate([xc[index][:width] for index in range(n_feat)], axis=0)
-    cot_full = jnp.concatenate([xc[index][width:] for index in range(n_feat)], axis=0)
-    qg[0, :width] = dot(wq_cols, x_full, 0, 0).astype(BF)
-    qg[0, width:] = (alive * dot(wo_rows, cot_full, 1, 0)).astype(BF)
-    qg_copy = send(qg.at[0], qg.at[1], qg_sem, 0, (partner, feat))
-    sent.append(qg_copy)
+    sent += ct_copies[1:] + rep_copies[1:] + xc_copies[1:]
+
+    for step in range(1, n_feat):
+        xg_copies[step].wait_recv()
+    qg[0, :width] = dot(wq_cols, xg[...].reshape(n_feat * width, rows), 0, 0).astype(BF)
 
     empty = jnp.full((1, 1), float(CENTROIDS), F32)
     for step in range(n_dom):
@@ -193,6 +194,23 @@
         empty = empty - jnp.sum(rep[step, 0:1, :], axis=1, keepdims=True)
     rep_cols = [column(rep[2 * step, 0:1, :]) for step in range(n_plane)]
 
+    for step in range(1, n_feat):
+        ct_copies[step].wait_recv()
+    cent_full = ct[...].reshape(n_feat * width, rows)
+    kvb[0] = dot(cent_full, wkv, 0, 0).astype(BF)
+    kv_copies = [None]
+    for step in range(1, n_plane):
+        kv_copies.append(
+            send(kvb.at[0], kvb.at[step], kv_sem, step, (dom_at(2 * step), feat))
+        )
+    sent += kv_copies[1:]
+
+    for step in range(1, n_feat):
+        xc_copies[step].wait_recv()
+    cot_full = xc[...].reshape(n_feat * width, rows)
+    qg[0, width:] = (alive * dot(wo_rows, cot_full, 1, 0)).astype(BF)
+    qg_copy = send(qg.at[0], qg.at[1], qg_sem, 0, (partner, feat))
+    sent.append(qg_copy)
     qg_copy.wait_recv()
     qg_all = jnp.concatenate([qg[0], qg[1]], axis=1)
     blank = jnp.zeros((width, 2 * rows), BF)
@@ -201,17 +219,6 @@
     q_low = q_rows.T
     g_high = g_rows.T
     low_lane = lax.broadcasted_iota(jnp.int32, (1, 2 * width), 1) < width
-
-    for step in range(1, n_feat):
-        ct_copies[step].wait_recv()
-    cent_full = ct[...].reshape(n_feat * width, rows)
-    kvb[0] = dot(cent_full, wkv, 0, 0).astype(BF)
-    kv_copies = [None]
-    for step in range(1, n_plane):
-        kv_copies.append(
-            send(kvb.at[0], kvb.at[step], kv_sem, step, (dom_at(2 * step), feat))
-        )
-    sent += kv_copies[1:]
 
     tops, zs, ds = [], [], []
     for step in range(n_plane):
@@ -272,36 +279,35 @@
     ap_copy = send(aqs, aqr, ap_sem, 0, (partner, feat))
     sent.append(ap_copy)
     ap_copy.wait_recv()
-    aq[feat] = (totals[:, :rows] + aqr[...]).astype(BF)
+    whole = (totals[:, :rows] + aqr[...]).astype(BF)
+    aq[feat] = whole[width:]
     aq_copies = [None]
     for step in range(1, n_feat):
         aq_copies.append(
             send(aq.at[feat], aq.at[feat], aq_sem, step, (dom, feat_at(step)))
         )
+    grad = dot(wq_cols, whole[:width], 1, 0)
     for step in range(1, n_plane):
         gr_copies[step].wait_recv()
         kv_own = kv_own + grecv[step].astype(F32)
-    kg[feat] = kv_own.astype(BF)
-    kg_copies = [None]
-    for step in range(1, n_feat):
-        kg_copies.append(
-            send(kg.at[feat], kg.at[feat], kg_sem, step, (dom, feat_at(step)))
-        )
-    sent += aq_copies[1:] + kg_copies[1:]
+    grad = grad + (alive / inv_count) * dot(wkv, kv_own.astype(BF), 1, 1)
+    grad = grad.reshape(n_feat, width, rows)
+    part[...] = grad
+    gp[...] = grad.astype(BF)
+    gp_copies = [None]
+    for step in range(1, n_feat):
+        target = feat_at(step)
+        gp_copies.append(send(gp.at[target], gpr.at[step], gp_sem, step, (dom, target)))
+    sent += aq_copies[1:] + gp_copies[1:]
     for step in range(1, n_feat):
         aq_copies[step].wait_recv()
-    gq_full = jnp.concatenate([aq[index][:width] for index in range(n_feat)], axis=0)
-    att_full = jnp.concatenate([aq[index][width:] for index in range(n_feat)], axis=0)
+    att_full = aq[...].reshape(n_feat * width, rows)
     out_ref[...] = (alive * dot(wo_cols, att_full, 0, 0)).astype(BF)
-    grad = dot(wq_rows, gq_full, 1, 0)
-    for step in range(1, n_feat):
-        kg_copies[step].wait_recv()
-    cent_grad = jnp.zeros((width, rows), F32)
-    for index in range(n_feat):
-        spot = slice(index * width, (index + 1) * width)
-        stacked = jnp.concatenate([wk_rows[:, spot], wv_rows[:, spot]], axis=1)
-        cent_grad = cent_grad + dot(stacked, kg[index], 1, 1)
-    gx_ref[...] = (grad + alive * (cent_grad / inv_count)).astype(BF)
+    total = part[feat]
+    for step in range(1, n_feat):
+        gp_copies[step].wait_recv()
+        total = total + gpr[step].astype(F32)
+    gx_ref[...] = total.astype(BF)
     for copy in sent:
         copy.wait_send()
 
@@ -327,7 +333,7 @@
         scratch_shapes=[
             pltpu.VMEM((n_dom, width, rows), BF),
             pltpu.VMEM((n_dom, 8, rows), F32),
-            pltpu.VMEM((n_feat, pair, rows), BF),
+            pltpu.VMEM((n_feat, width, rows), BF),
             pltpu.VMEM((n_feat, width, rows), BF),
             pltpu.VMEM((n_dom, 8, rows), F32),
             pltpu.VMEM((n_plane, rows, pair), BF),
@@ -337,8 +343,11 @@
             pltpu.VMEM((n_plane, rows, pair), BF),
             pltpu.VMEM((pair, rows), F32),
             pltpu.VMEM((pair, rows), F32),
-            pltpu.VMEM((n_feat, rows, pair), BF),
-            pltpu.VMEM((n_feat, pair, rows), BF),
+            pltpu.VMEM((n_feat, width, rows), BF),
+            pltpu.VMEM((n_feat, width, rows), BF),
+            pltpu.VMEM((n_feat, width, rows), F32),
+            pltpu.VMEM((n_feat, width, rows), BF),
+            pltpu.VMEM((n_feat, width, rows), BF),
             pltpu.VMEM((n_plane, rows, 2 * rows), F32),
             pltpu.VMEM((n_plane, rows, 2 * rows), F32),
             sems(n_dom),
@@ -351,6 +360,7 @@
             sems(1),
             sems(n_plane),
             sems(1),
+            sems(n_feat),
             sems(n_feat),
             sems(n_feat),
         ],

time: 44 us -> 39.3 us (0.89)
  Pallas kernels: 40.5 us -> 35.8 us
    pallas_call x1, Pallas kernels: 40.5 us -> 35.8 us  [fused(): pl.pallas_call(functools.partial(kernel, n_dom, n_feat), out_shape=(jax.S...]
where the time goes in v3:
time: 39.3 us; the launch traced here: 39.1 us
  Pallas kernels  35.8 us (91%)
  local copies, waits for them, and re-layouts  2 us (5%)
  between operations  1.29 us (3%)
    pallas_call x1, Pallas kernels, fused(): pl.pallas_call(functools.partial(kernel, n_dom, n_feat), out_shape=(jax.S...  35.8 us
    unnamed x4, local copies, waits for them, and re-layouts  2 us

profile of v3, /device:TPU:0, one launch (start us, length us, event | category | flops | bytes accessed | tf_op | source)
XLA Modules:
  0.0 39.1 jit_solution(3586601093500248144)
XLA Ops:
  1.3 35.8 %shard_map.95 = (bf16[64,256]{1,0:T(8,128)(2,1)}, bf16[64,256]{1,0:T(8,128)(2,1)}) custom-call(bf16[64,256]{1,0:T(8,128)(2,1)} %bitcast.7, bf16[64,256]{1,0:T(8,128)(2,1)} %bitcast.8, s32[1,256]{1,0:T(1,128)} %bitcast.9, s32[1]{0:T(128)S(6)} %copy.12.size_ref, bf16[256,256]{1,0:T(8,128)(2,1)} %wq_ref.1, bf16[256,256]{1,0:T(8,128)(2,1)} %wk_ref.1, ...), custom_call_target="tpu_custom_call" | custom-call | tf_op jit(solution)/shard_map/pallas_call | solution.py:325
  37.1 0.0 copy-start
  37.1 1.4 %copy.13 = bf16[256,64]{0,1:T(8,128)(2,1)} copy(bf16[256,64]{0,1:T(8,128)(2,1)} %bitcast.6) | data formatting | bytes 65536
  38.5 0.0 copy-done
  38.5 0.6 %copy.14 = bf16[256,64]{0,1:T(8,128)(2,1)} copy(bf16[256,64]{0,1:T(8,128)(2,1)S(1)} %bitcast.5) | data formatting | bytes 65536
Async XLA Ops:
  37.1 1.4 %copy-start = (bf16[64,256]{1,0:T(8,128)(2,1)S(1)}, bf16[64,256]{1,0:T(8,128)(2,1)}, u32[]{:S(2)}) copy-start(bf16[64,256]{1,0:T(8,128)(2,1)} %get-tuple-element.5) | copy-start | bytes 98308

commit v4 on v3

--- a/solution.py
+++ b/solution.py
@@ -32,7 +32,6 @@
     wv_ref,
     wo_ref,
     out_ref,
-    gx_ref,
     xp,
     am,
     xc,
@@ -52,6 +51,8 @@
     gpr,
     e_buf,
     g_buf,
+    masked,
+    low_buf,
     xp_sem,
     am_sem,
     xc_sem,
@@ -77,6 +78,20 @@
     def dom_at(step):
         return lax.rem(dom + step + n_dom, n_dom)
 
+    def source(step):
+        if n_plane == 4:
+            plane = dom // 2
+            across, along = plane // 2, lax.rem(plane, 2)
+            if step != 3:
+                across = 1 - across
+            if step != 2:
+                along = 1 - along
+            return 4 * across + 2 * along + core
+        return dom_at(-2 * step)
+
+    def reader(step):
+        return source(step) if n_plane == 4 else dom_at(2 * step)
+
     def feat_at(step):
         return lax.rem(feat + step + n_feat, n_feat)
 
@@ -192,7 +207,10 @@
         if step:
             rep_copies[step].wait_recv()
         empty = empty - jnp.sum(rep[step, 0:1, :], axis=1, keepdims=True)
-    rep_cols = [column(rep[2 * step, 0:1, :]) for step in range(n_plane)]
+    rep_cols = [column(rep[0, 0:1, :])]
+    for step in range(1, n_plane):
+        slot = lax.rem(dom - source(step) + n_dom, n_dom)
+        rep_cols.append(column(rep[slot, 0:1, :]))
 
     for step in range(1, n_feat):
         ct_copies[step].wait_recv()
@@ -201,7 +219,7 @@
     kv_copies = [None]
     for step in range(1, n_plane):
         kv_copies.append(
-            send(kvb.at[0], kvb.at[step], kv_sem, step, (dom_at(2 * step), feat))
+            send(kvb.at[0], kvb.at[step], kv_sem, step, (reader(step), feat))
         )
     sent += kv_copies[1:]
 
@@ -245,6 +263,10 @@
     st[0, 3:8, :] = jnp.zeros((5, 2 * rows), F32)
     st_copy = send(st.at[0], st.at[1], st_sem, 0, (partner, feat))
     sent.append(st_copy)
+    for step in range(n_plane):
+        kv = kvb[step].astype(F32) * rep_cols[step]
+        masked[0, :, step * rows : (step + 1) * rows] = jnp.where(low_lane, kv, 0.0).astype(BF).T
+        masked[1, :, step * rows : (step + 1) * rows] = jnp.where(low_lane, 0.0, kv).astype(BF).T
     st_copy.wait_recv()
     other = st[1]
     other = jnp.concatenate([other[:, rows:], other[:, :rows]], axis=1)
@@ -254,7 +276,6 @@
     z_all = z_own * own_fix + other[1:2] * other_fix + empty * jnp.exp(-top_all)
     delta = (d_own * own_fix + other[2:3] * other_fix) / z_all
 
-    totals = jnp.zeros((2 * width, 2 * rows), F32)
     gr_copies = [None] * n_plane
     kv_own = None
     for step in list(range(1, n_plane)) + [0]:
@@ -262,18 +283,17 @@
         probs = e_buf[step] * scale
         probs_low = probs.astype(BF)
         g_scores = (probs * (g_buf[step] - delta) * inv_root).astype(BF)
+        low_buf[0, step * rows : (step + 1) * rows, :] = g_scores
+        low_buf[1, step * rows : (step + 1) * rows, :] = probs_low
         partial = dot(g_scores, q_low, 1, 0) + dot(probs_low, g_high, 1, 0)
         if step:
             gsend[step] = partial.astype(BF)
             gr_copies[step] = send(
-                gsend.at[step], grecv.at[step], gr_sem, step, (dom_at(-2 * step), feat)
+                gsend.at[step], grecv.at[step], gr_sem, step, (source(step), feat)
             )
         else:
             kv_own = partial
-        kv = kvb[step].astype(F32) * rep_cols[step]
-        k_low = jnp.where(low_lane, kv, 0.0).astype(BF)
-        v_high = jnp.where(low_lane, 0.0, kv).astype(BF)
-        totals = totals + dot(k_low, g_scores, 0, 0) + dot(v_high, probs_low, 0, 0)
+    totals = dot(masked[0], low_buf[0], 1, 0) + dot(masked[1], low_buf[1], 1, 0)
     sent += gr_copies[1:]
     aqs[...] = totals[:, rows:]
     ap_copy = send(aqs, aqr, ap_sem, 0, (partner, feat))
@@ -302,12 +322,12 @@
     for step in range(1, n_feat):
         aq_copies[step].wait_recv()
     att_full = aq[...].reshape(n_feat * width, rows)
-    out_ref[...] = (alive * dot(wo_cols, att_full, 0, 0)).astype(BF)
+    out_ref[:width] = (alive * dot(wo_cols, att_full, 0, 0)).astype(BF)
     total = part[feat]
     for step in range(1, n_feat):
         gp_copies[step].wait_recv()
         total = total + gpr[step].astype(F32)
-    gx_ref[...] = total.astype(BF)
+    out_ref[width:] = total.astype(BF)
     for copy in sent:
         copy.wait_send()
 
@@ -322,14 +342,11 @@
     def sems(count):
         return pltpu.SemaphoreType.DMA((2, count))
 
-    out, grad = pl.pallas_call(
+    both = pl.pallas_call(
         functools.partial(kernel, n_dom, n_feat),
-        out_shape=(
-            jax.ShapeDtypeStruct((width, rows), BF),
-            jax.ShapeDtypeStruct((width, rows), BF),
-        ),
+        out_shape=jax.ShapeDtypeStruct((pair, rows), BF),
         in_specs=[vmem, vmem, vmem, smem, vmem, vmem, vmem, vmem],
-        out_specs=(vmem, vmem),
+        out_specs=vmem,
         scratch_shapes=[
             pltpu.VMEM((n_dom, width, rows), BF),
             pltpu.VMEM((n_dom, 8, rows), F32),
@@ -350,6 +367,8 @@
             pltpu.VMEM((n_feat, width, rows), BF),
             pltpu.VMEM((n_plane, rows, 2 * rows), F32),
             pltpu.VMEM((n_plane, rows, 2 * rows), F32),
+            pltpu.VMEM((2, pair, n_plane * rows), BF),
+            pltpu.VMEM((2, n_plane * rows, 2 * rows), BF),
             sems(n_dom),
             sems(n_dom),
             sems(n_feat),
@@ -375,7 +394,7 @@
         w_value,
         w_out,
     )
-    return out.T, grad.T
+    return both[:width].T, both[width:].T
 
 
 def trans_dot(left, right):

time: 39.3 us -> 38.2 us (0.972)
  local copies, waits for them, and re-layouts: 2 us -> 1.4 us
  Pallas kernels: 35.8 us -> 35.3 us
    unnamed x4 -> x0, local copies, waits for them, and re-layouts: 2 us -> none
    transpose x0 -> x1, local copies, waits for them, and re-layouts: none -> 1.4 us  [fused(): return (both[:width].T, both[width:].T)]
    pallas_call x1, Pallas kernels: 35.8 us -> 35.3 us  [fused(): pl.pallas_call(functools.partial(kernel, n_dom, n_feat), out_shape=jax.Sh...]
where the time goes in v4:
time: 38.2 us; the launch traced here: 38 us
  Pallas kernels  35.3 us (92%)
  local copies, waits for them, and re-layouts  1.4 us (4%)
  between operations  1.29 us (3%)
    pallas_call x1, Pallas kernels, fused(): pl.pallas_call(functools.partial(kernel, n_dom, n_feat), out_shape=jax.Sh...  35.3 us
    transpose x1, local copies, waits for them, and re-layouts, fused(): return (both[:width].T, both[width:].T)  1.4 us

profile of v4, /device:TPU:0, one launch (start us, length us, event | category | flops | bytes accessed | tf_op | source)
XLA Modules:
  0.0 38.0 jit_solution(6097342320339833487)
XLA Ops:
  1.3 35.3 %shard_map.95 = bf16[128,256]{1,0:T(8,128)(2,1)} custom-call(bf16[64,256]{1,0:T(8,128)(2,1)} %bitcast.7, bf16[64,256]{1,0:T(8,128)(2,1)} %bitcast.8, s32[1,256]{1,0:T(1,128)} %bitcast.9, s32[1]{0:T(128)S(6)} %copy.10.size_ref, bf16[256,256]{1,0:T(8,128)(2,1)} %wq_ref.1, bf16[256,256]{1,0:T(8,128)(2,1)} %wk_ref.1, bf16[256,256]{1,0:T(8,128)(2,1)} %wv_ref.1, ...), custom_call_target="tpu_custom_call" | custom-call | tf_op jit(solution)/shard_map/pallas_call | solution.py:345
  36.6 1.4 %slice_bitcast_fusion = (bf16[256,64]{0,1:T(8,128)(2,1)}, bf16[256,64]{0,1:T(8,128)(2,1)}) fusion(bf16[128,256]{1,0:T(8,128)(2,1)} %shard_map.95), kind=kLoop, calls=%fused_computation | loop fusion | bytes 131072 | tf_op jit(solution)/shard_map/transpose | solution.py:397
